TPU v7x, 256 devices: a whole 4x4x8 slice. The times are simulated.
256 devices in a mesh: ind: 64 (over z_hi, y, x, core), snp: 4 (over z_lo).
Axes of the slice: x: 4, y: 4, z: 8 (z_hi: 2, z_lo: 4; z = z_hi * 4 + z_lo), core: 2. Of those that a mesh axis runs over, the one named last changes fastest.
Arguments:
- dosages: bfloat16 [11264, 131072], P('ind', 'snp'), may hold values from 0 to 2, as said below
- phenotype: int32 [11264], P('ind'), may hold values 0 or 1
- mean_effect: float32 [131072], P(('snp', 'ind')), may hold values from -3 to 3
- factor: float32 [131072, 256], P(('snp', 'ind')), may hold values from -1 to 1
- log_scale: float32 [131072], P(('snp', 'ind')), may hold values from -1 to 0
- diag_noise: float32 [131072, 128], P(('snp', 'ind')), may hold values from -5 to 5
- base_points: float32 [128, 256], replicated, may hold values from -5 to 5
Outputs:
- grad_mean: float32 [131072], P(('snp', 'ind'))
- grad_factor: float32 [131072, 256], P(('snp', 'ind'))
- grad_log_scale: float32 [131072], P(('snp', 'ind'))
- mean_loglik: float32 [], replicated
- rank_entropy: float32 [], replicated
Inputs may be any that keep to these rules, and one draw needn't show every extreme that they name: `dosages`: each entry is an allele count.
All inputs are finite; a program needn't handle non-finite values. No bound on the sum of `phenotype` on one device may be relied on, other than what follows from the above.
Results may differ from a plain program's by a relative error of at most 0.00085.
The roundings to bfloat16 on the way count: a program that leaves them out, or rounds other values in their place, can miss the bound.
Values may be sent and summed in bfloat16 or wider, within the bound.
No kernel may reach another device: no remote copies, remote signals or barrier semaphores. Data moves between devices by JAX's collectives and lax.ppermute only.
A program may use at most 128 MiB of HBM per device.

v0:
```python
import math
import jax
import jax.numpy as jnp
from jax import lax
from jax.sharding import PartitionSpec as P

P_SIZE = 131072
R = 256
S = 128
COHORT_RATIO = 40


def invert_gram(gram_matrix):
    factor_chol = jnp.linalg.cholesky(gram_matrix)
    identity = jnp.eye(gram_matrix.shape[0], dtype=gram_matrix.dtype)
    lower_inv = lax.linalg.triangular_solve(factor_chol, identity, left_side=True, lower=True)
    inverse = jnp.dot(lower_inv.T, lower_inv, precision=lax.Precision.HIGHEST)
    return (factor_chol, inverse)


def on_device(dosages, phenotype, mean_effect, factor, log_scale, diag_noise, base_points):
    sample_count = base_points.shape[0]
    local_ind = dosages.shape[0]
    total_ind = local_ind * lax.axis_size("ind")
    root_p = math.sqrt(P_SIZE)
    spread = jnp.exp(log_scale)
    low_rank = jnp.dot(factor, base_points.T, precision=lax.Precision.HIGHEST)
    samples = ((mean_effect[:, None] + low_rank + spread[:, None] * diag_noise) / root_p).astype(
        jnp.bfloat16
    )
    columns = dosages
    partial_logits = jnp.dot(
        columns,
        lax.all_gather(samples, "ind", axis=0, tiled=True),
        preferred_element_type=jnp.float32,
    )
    labels = phenotype.astype(jnp.float32)[:, None]
    logits = lax.psum(partial_logits.astype(jnp.bfloat16), "snp").astype(jnp.float32)
    loglik_terms = jnp.sum(labels * logits - jax.nn.softplus(logits))
    loglik_total = lax.psum(loglik_terms, "ind")
    weights = (COHORT_RATIO * (labels - jax.nn.sigmoid(logits)) / S).astype(jnp.bfloat16)
    mean_loglik = loglik_total / (total_ind * sample_count)
    columns = dosages
    gradient = lax.psum_scatter(
        lax.dot_general(
            columns, weights, (((0,), (0,)), ((), ())), preferred_element_type=jnp.float32
        ),
        "ind",
        scatter_dimension=0,
        tiled=True,
    )
    scaled = factor / spread[:, None]
    identity = jnp.eye(R, dtype=jnp.float32)
    gram_part = jnp.dot(scaled.T, scaled, precision=lax.Precision.HIGHEST)
    gram_matrix = identity + lax.psum(gram_part, ("ind", "snp"))
    factor_chol, inverse = invert_gram(gram_matrix)
    rank_entropy = jnp.sum(jnp.log(jnp.diagonal(factor_chol))) / R
    projected = jnp.dot(factor, inverse, precision=lax.Precision.HIGHEST)
    spread_sq = spread * spread
    grad_mean = jnp.sum(gradient, axis=1) / root_p - mean_effect
    grad_factor = (
        jnp.dot(gradient, base_points, precision=lax.Precision.HIGHEST) / root_p
        - factor
        + projected / spread_sq[:, None]
    )
    leverage = jnp.sum(projected * factor, axis=1)
    grad_log_scale = (
        spread * jnp.sum(gradient * diag_noise, axis=1) / root_p
        + 1.0
        - spread_sq
        - leverage / spread_sq
    )
    return (grad_mean, grad_factor, grad_log_scale, mean_loglik, rank_entropy)


def solution(mesh):
    in_specs = (
        P("ind", "snp"),
        P("ind"),
        P(("snp", "ind")),
        P(("snp", "ind"), None),
        P(("snp", "ind")),
        P(("snp", "ind"), None),
        P(),
    )
    out_specs = (P(("snp", "ind")), P(("snp", "ind"), None), P(("snp", "ind")), P(), P())
    return jax.shard_map(
        on_device, mesh=mesh, in_specs=in_specs, out_specs=out_specs, check_vma=False
    )
```

profile of v0, /device:TPU:32, one launch (start us, length us, event | category | flops | bytes accessed | tf_op | source)
XLA Modules:
  0.0 618.1 jit_solution(5039435738711736244)
XLA Ops:
  8.1 0.7 exp.10
  8.9 2.4 fusion.4
  11.3 3.1 fusion.6
  14.5 0.7 convert_element_type.24
  15.2 112.5 %all-gather.2.cloned.1.call-done = bf16[32768,128]{1,0:T(8,128)(2,1)} async-done(((bf16[512,128]{1,0:T(8,128)(2,1)}), bf16[32768,128]{1,0:T(8,128)(2,1)}) %all-gather.2.cloned.1.call-update) | async-done | bytes 8388624 | tf_op jit(solution)/shard_map/all_gather | solution.py:34
  127.6 9.9 %fusion.5 = bf16[176,128]{1,0:T(8,128)(2,1)S(1)} fusion(bf16[176,32768]{1,0:T(8,128)(2,1)} %param.7, bf16[32768,128]{1,0:T(8,128)(2,1)} %all-gather.2.cloned.1.call-done), kind=kOutput, calls=%fused_computation.15 | convolution fusion | flops 1476417536 | bytes 19968000 | tf_op jit(solution)/shard_map/dot_general | solution.py:32
  137.5 15.6 %psum.21 = bf16[176,128]{1,0:T(8,128)(2,1)S(1)} all-reduce(bf16[176,128]{1,0:T(8,128)(2,1)S(1)} %fusion.5), channel_id=1, replica_groups=mesh['ind'=64,'snp'=4] {'snp'}, use_global_device_ids=true, to_apply=%region_0.0 | all-reduce | flops 22528 | bytes 90112 | tf_op jit(solution)/shard_map/psum | solution.py:38
  153.1 12.5 %convolution_bitcast_fusion = f32[32768,128]{0,1:T(8,128)} fusion(bf16[176,32768]{1,0:T(8,128)(2,1)} %param.7, bf16[176,128]{1,0:T(8,128)(2,1)S(1)} %psum.21, f32[176]{0:T(256)S(1)} %convert_element_type.24), kind=kOutput, calls=%fused_computation.3 | convolution fusion | flops 1476552704 | bytes 28357312 | tf_op jit(solution)/shard_map/dot_general | solution.py:45
  165.6 0.9 copy-done.2
  166.7 122.0 %all-reduce.3.cloned.1.call-done = f32[256,256]{0,1:T(8,128)} async-done(((f32[256,256]{0,1:T(8,128)}), f32[256,256]{0,1:T(8,128)}) %all-reduce.3.cloned.1.call-update) | async-done | bytes 262160 | tf_op jit(solution)/shard_map/psum | solution.py:55
  288.7 1.0 convert_add_fusion
  289.8 1.0 fusion.12
  290.8 11.7 %cholesky.50 = f32[128,128]{1,0:T(8,128)S(1)} custom-call(f32[128,128]{1,0:T(8,128)S(1)} %cholesky.118), custom_call_target="Cholesky" | custom-call | tf_op jit(solution)/shard_map/jit(cholesky)/cholesky | solution.py:14
  302.6 9.8 %custom-call.14 = f32[1,128,128]{1,2,0:T(8,128)S(1)} custom-call(f32[1,128,128]{2,1,0:T(8,128)S(1)} %get-tuple-element.30), custom_call_target="InvertDiagBlocksLowerTriangular" | custom-call | tf_op jit(solution)/shard_map/jit(cholesky)/cholesky | solution.py:14
  312.9 11.9 %cholesky.105 = f32[128,128]{1,0:T(8,128)S(1)} custom-call(f32[128,128]{1,0:T(8,128)S(1)} %convolution_subtract_fusion.1), custom_call_target="Cholesky" | custom-call | tf_op jit(solution)/shard_map/jit(cholesky)/cholesky | solution.py:14
  324.8 0.6 compare_reduce_fusion.1
  325.5 0.6 compare_reduce_fusion
  327.5 4.0 while.1
  327.5 0.6 fusion.57
  328.1 1.4 bitcast_dynamic-update-slice_fusion.2
  330.1 1.4 bitcast_dynamic-update-slice_fusion.2
  331.5 19.7 %custom-call.15 = f32[2,128,128]{1,2,0:T(8,128)S(1)} custom-call(f32[2,128,128]{2,1,0:T(8,128)S(1)} %get-tuple-element.12), custom_call_target="InvertDiagBlocksLowerTriangular" | custom-call | tf_op jit(solution)/shard_map/triangular_solve | solution.py:16
  351.2 2.3 gather_fusion
  353.6 0.6 log_reduce_fusion
  355.1 0.6 fusion.8
  355.8 0.7 multiply_reduce_fusion
  356.4 0.7 fusion.25
  357.8 208.4 %psum.23 = f32[]{:T(128)} all-reduce(f32[]{:T(128)} %fusion.25), channel_id=1, replica_groups=mesh['ind'=64,'snp'=4] {'ind'}, use_global_device_ids=true, to_apply=%region_11.12 | all-reduce | flops 1 | bytes 8 | tf_op jit(solution)/shard_map/psum | solution.py:40
  566.9 37.5 %reduce-scatter.2.cloned.1.call-done = f32[512,128]{0,1:T(8,128)} async-done(((f32[32768,128]{0,1:T(8,128)}), f32[512,128]{0,1:T(8,128)}) %reduce-scatter.2.cloned.1.call-update) | async-done | bytes 262160 | tf_op jit(solution)/shard_map/reduce_scatter | solution.py:44
  604.4 1.0 multiply_reduce_fusion.1
  605.4 0.6 divide_subtract_fusion
  606.0 2.4 fusion.1
  (36 shorter events, 2.9 us)
Async XLA Ops:
  8.0 0.9 copy-start
  8.0 119.6 %all-gather.2.cloned.1.call-start = ((), (), s32[]{:S(2)}) async-start(), calls=%async_computation.1 | async-start | bytes 8519680 | tf_op jit(solution)/shard_map/all_gather | solution.py:34
  11.3 277.4 %all-reduce.3.cloned.1.call-start = ((), (), s32[]{:S(2)}) async-start(), calls=%async_computation.3 | async-start | bytes 524288 | tf_op jit(solution)/shard_map/psum | solution.py:55
  14.4 589.9 %reduce-scatter.2.cloned.1.call-start = ((), (), s32[]{:S(2)}) async-start(), calls=%async_computation.2 | async-start | bytes 17039360 | tf_op jit(solution)/shard_map/reduce_scatter | solution.py:44
  165.6 0.9 copy-start.2
  165.6 190.2 %copy-start.1 = (f32[512,256]{1,0:T(8,128)S(1)}, f32[512,256]{1,0:T(8,128)}, u32[]{:S(2)}) copy-start(f32[512,256]{1,0:T(8,128)} %param.10) | copy-start | bytes 1572868
  165.6 439.8 %copy-start.3 = (f32[512]{0:T(512)S(1)}, f32[512]{0:T(512)}, u32[]{:S(2)}) copy-start(f32[512]{0:T(512)} %param.9) | copy-start | bytes 6148
  165.6 439.8 %copy-start.4 = (f32[512]{0:T(512)S(1)}, f32[512]{0:T(512)}, u32[]{:S(2)}) copy-start(f32[512]{0:T(512)} %param.11) | copy-start | bytes 6148
Sparse Core Ops, SparseCore 0:
  12.5 115.0 all-gather.1
  165.7 438.5 reduce-scatter.1
Sparse Core Ops, SparseCore 1:
  17.8 270.9 all-reduce.2
where the time goes:
time: 619 us; the launch traced here: 618 us
  waiting for transfers between devices  272 us (44%)
  blocking collectives  224 us (36%)
  other arithmetic  60.1 us (10%)
  matrix products  32.9 us (5%)
  between operations  20.6 us (3%)
  local copies, waits for them, and re-layouts  8.42 us (1%)
    psum x1, blocking collectives, on_device(): loglik_total = lax.psum(loglik_terms, 'ind')  208 us
    psum x1, waiting for transfers between devices, on_device(): gram_matrix = identity + lax.psum(gram_part, ('ind', 'snp'))  122 us
    all_gather x1, waiting for transfers between devices, on_device(): lax.all_gather(samples, 'ind', axis=0, tiled=True)  112 us
    reduce_scatter x1, waiting for transfers between devices, on_device(): lax.psum_scatter(lax.dot_general(columns, weights, (((0,), (0,)), ((), ()...  37.5 us
    another operation x7, other arithmetic, invert_gram(): factor_chol = jnp.linalg.cholesky(gram_matrix)  34.8 us
    another operation x3, other arithmetic, invert_gram(): lax.linalg.triangular_solve(factor_chol, identity, left_side=True, lower=...  19.7 us
    psum x1, blocking collectives, on_device(): lax.psum(partial_logits.astype(jnp.bfloat16), 'snp').astype(jnp.float32)  15.6 us
    dot_general x1, matrix products, on_device(): lax.dot_general(columns, weights, (((0,), (0,)), ((), ())), preferred_ele...  12.5 us
  transfers between devices with their start and end apart: 3, of which 3 were waited for; matrix products, arithmetic and copies ran while one was open for 15% of the time, Pallas kernels for 0%

commit v1 on v0

--- a/solution.py
+++ b/solution.py
@@ -52,7 +52,7 @@
     scaled = factor / spread[:, None]
     identity = jnp.eye(R, dtype=jnp.float32)
     gram_part = jnp.dot(scaled.T, scaled, precision=lax.Precision.HIGHEST)
-    gram_matrix = identity + lax.psum(gram_part, ("ind", "snp"))
+    gram_matrix = identity + lax.psum(lax.psum(gram_part, "snp"), "ind")
     factor_chol, inverse = invert_gram(gram_matrix)
     rank_entropy = jnp.sum(jnp.log(jnp.diagonal(factor_chol))) / R
     projected = jnp.dot(factor, inverse, precision=lax.Precision.HIGHEST)

time: 619 us -> 1320 us (2.13)
  waiting for transfers between devices: 272 us -> 972 us
    psum x1 -> x2, waiting for transfers between devices: 122 us -> 749 us  [on_device(): gram_matrix = identity + lax.psum(lax.psum(gram_part, 'snp'), 'ind')]
    reduce_scatter x1, waiting for transfers between devices: 37.5 us -> 160 us  [on_device(): lax.psum_scatter(lax.dot_general(columns, weights, (((0,), (0,)), ((), ()...]
    all_gather x1, waiting for transfers between devices: 112 us -> 62.6 us  [on_device(): lax.all_gather(samples, 'ind', axis=0, tiled=True)]
  transfers between devices with their start and end apart: 3 -> 4, of which waited for: 3 -> 4; matrix products, arithmetic and copies ran while one was open for 15% -> 7% of each run, Pallas kernels for 0% -> 0%
where the time goes in v1:
time: 1320 us
  waiting for transfers between devices  972 us (74%)
  blocking collectives  228 us (17%)
  other arithmetic  60.1 us (5%)
  matrix products  32.8 us (2%)
  between operations  20.7 us (2%)
    psum x2, waiting for transfers between devices, on_device(): gram_matrix = identity + lax.psum(lax.psum(gram_part, 'snp'), 'ind')  749 us
    psum x1, blocking collectives, on_device(): loglik_total = lax.psum(loglik_terms, 'ind')  212 us
    reduce_scatter x1, waiting for transfers between devices, on_device(): lax.psum_scatter(lax.dot_general(columns, weights, (((0,), (0,)), ((), ()...  160 us
    all_gather x1, waiting for transfers between devices, on_device(): lax.all_gather(samples, 'ind', axis=0, tiled=True)  62.6 us
    another operation x7, other arithmetic, invert_gram(): factor_chol = jnp.linalg.cholesky(gram_matrix)  34.8 us
  transfers between devices with their start and end apart: 4, of which 4 were waited for; matrix products, arithmetic and copies ran while one was open for 7% of the time, Pallas kernels for 0%

profile of v1, /device:TPU:32, one launch (start us, length us, event | category | flops | bytes accessed | tf_op | source)
XLA Modules:
  0.0 1321.9 jit_solution(16298854465886490964)
XLA Ops:
  8.1 0.7 exp.10
  8.8 3.1 fusion.6
  11.9 2.4 fusion.4
  14.4 0.7 convert_element_type.24
  15.1 53.9 %all-reduce.4.cloned.1.call-done = f32[256,256]{0,1:T(8,128)} async-done(((f32[256,256]{0,1:T(8,128)}), f32[256,256]{0,1:T(8,128)}) %all-reduce.4.cloned.1.call-update) | async-done | bytes 262160 | tf_op jit(solution)/shard_map/psum | solution.py:55
  69.0 62.6 %all-gather.2.cloned.1.call-done = bf16[32768,128]{1,0:T(8,128)(2,1)} async-done(((bf16[512,128]{1,0:T(8,128)(2,1)}), bf16[32768,128]{1,0:T(8,128)(2,1)}) %all-gather.2.cloned.1.call-update) | async-done | bytes 8388624 | tf_op jit(solution)/shard_map/all_gather | solution.py:34
  131.7 9.8 fusion.5
  141.5 15.6 %psum.28 = bf16[176,128]{1,0:T(8,128)(2,1)S(1)} all-reduce(bf16[176,128]{1,0:T(8,128)(2,1)S(1)} %fusion.5), channel_id=1, replica_groups=mesh['ind'=64,'snp'=4] {'snp'}, use_global_device_ids=true, to_apply=%region_0.0 | all-reduce | flops 22528 | bytes 90112 | tf_op jit(solution)/shard_map/psum | solution.py:38
  157.1 12.4 convolution_bitcast_fusion
  169.6 0.9 copy-done.2
  170.7 694.9 %all-reduce.6.cloned.1.call-done = f32[256,256]{0,1:T(8,128)} async-done(((f32[256,256]{0,1:T(8,128)}), f32[256,256]{0,1:T(8,128)}) %all-reduce.6.cloned.1.call-update) | async-done | bytes 262160 | tf_op jit(solution)/shard_map/psum | solution.py:55
  865.6 1.0 convert_add_fusion
  866.7 1.0 fusion.12
  867.8 11.7 cholesky.50
  879.5 9.8 custom-call.14
  889.8 11.9 cholesky.105
  901.7 0.6 compare_reduce_fusion.1
  902.4 0.6 compare_reduce_fusion
  904.5 4.0 while.1
  905.1 1.4 bitcast_dynamic-update-slice_fusion.2
  907.1 1.4 bitcast_dynamic-update-slice_fusion.2
  908.5 19.7 %custom-call.15 = f32[2,128,128]{1,2,0:T(8,128)S(1)} custom-call(f32[2,128,128]{2,1,0:T(8,128)S(1)} %get-tuple-element.12), custom_call_target="InvertDiagBlocksLowerTriangular" | custom-call | tf_op jit(solution)/shard_map/triangular_solve | solution.py:16
  928.1 2.3 gather_fusion
  930.5 0.6 log_reduce_fusion
  932.1 0.6 fusion.8
  932.7 0.7 multiply_reduce_fusion
  933.4 0.7 fusion.25
  934.7 212.2 %psum.31 = f32[]{:T(128)} all-reduce(f32[]{:T(128)} %fusion.25), channel_id=1, replica_groups=mesh['ind'=64,'snp'=4] {'ind'}, use_global_device_ids=true, to_apply=%region_12.13 | all-reduce | flops 1 | bytes 8 | tf_op jit(solution)/shard_map/psum | solution.py:40
  1147.5 160.5 %reduce-scatter.2.cloned.1.call-done = f32[512,128]{0,1:T(8,128)} async-done(((f32[32768,128]{0,1:T(8,128)}), f32[512,128]{0,1:T(8,128)}) %reduce-scatter.2.cloned.1.call-update) | async-done | bytes 262160 | tf_op jit(solution)/shard_map/reduce_scatter | solution.py:44
  1308.0 1.0 multiply_reduce_fusion.1
  1309.0 0.6 divide_subtract_fusion
  1309.6 2.4 fusion.1
  (39 shorter events, 3.4 us)
Async XLA Ops:
  8.0 3.9 copy-start
  8.0 60.9 %all-reduce.4.cloned.1.call-start = ((), (), s32[]{:S(2)}) async-start(), calls=%async_computation.3 | async-start | bytes 524288 | tf_op jit(solution)/shard_map/psum | solution.py:55
  11.9 119.8 %all-gather.2.cloned.1.call-start = ((), (), s32[]{:S(2)}) async-start(), calls=%async_computation.1 | async-start | bytes 8519680 | tf_op jit(solution)/shard_map/all_gather | solution.py:34
  14.3 851.3 %all-reduce.6.cloned.1.call-start = ((), (), s32[]{:S(2)}) async-start(), calls=%async_computation.4 | async-start | bytes 524288 | tf_op jit(solution)/shard_map/psum | solution.py:55
  69.0 1239.1 %reduce-scatter.2.cloned.1.call-start = ((), (), s32[]{:S(2)}) async-start(), calls=%async_computation.2 | async-start | bytes 17039360 | tf_op jit(solution)/shard_map/reduce_scatter | solution.py:44
  169.6 0.9 copy-start.2
  169.6 763.1 %copy-start.1 = (f32[512,256]{1,0:T(8,128)S(1)}, f32[512,256]{1,0:T(8,128)}, u32[]{:S(2)}) copy-start(f32[512,256]{1,0:T(8,128)} %param.10) | copy-start | bytes 1572868
  169.6 1139.5 %copy-start.3 = (f32[512]{0:T(512)S(1)}, f32[512]{0:T(512)}, u32[]{:S(2)}) copy-start(f32[512]{0:T(512)} %param.9) | copy-start | bytes 6148
  169.6 1139.5 %copy-start.4 = (f32[512]{0:T(512)S(1)}, f32[512]{0:T(512)}, u32[]{:S(2)}) copy-start(f32[512]{0:T(512)} %param.11) | copy-start | bytes 6148
Sparse Core Ops, SparseCore 0:
  12.1 56.8 all-reduce.3
Sparse Core Ops, SparseCore 1:
  16.0 115.6 all-gather.1
  134.3 731.2 all-reduce.5
  868.1 439.9 reduce-scatter.1
